TPU v7x, 256 devices: a whole 4x4x8 slice. The times are simulated.
256 devices in a mesh: dp: 16 (over z_lo, x), seq: 16 (over z_hi, y, core).
Axes of the slice: x: 4, y: 4, z: 8 (z_hi: 2, z_lo: 4; z = z_hi * 4 + z_lo), core: 2. Of those that a mesh axis runs over, the one named last changes fastest.
Arguments:
- queries: bfloat16 [16, 2048, 2048], P('dp', 'seq'), may hold values from -5 to 5
- key_states: bfloat16 [16, 2048, 2048], P('dp', 'seq'), may hold values from -5 to 5
- value_states: bfloat16 [16, 2048, 2048], P('dp', 'seq'), may hold values from -6 to 6
- residual: bfloat16 [16, 2048, 2048], P('dp', 'seq'), may hold values from -6 to 6
- enc_hidden: bfloat16 [16, 2048, 1536], P('dp', 'seq'), may hold values from -6 to 6
- enc_gain: float32 [1536], replicated, may hold values from 0.1 to 1.9
- enc_bias: float32 [1536], replicated, may hold values from -0.5 to 0.5
- feature_target: int32 [16, 2048], P('dp', 'seq'), may hold values from 0 to 2047, as said below
- timestep: int32 [16], P('dp'), may hold values from 0 to 999
- gate_weight: bfloat16 [256, 2048], P('dp'), may hold values from -0.375 to 0.375
- lift_weight: bfloat16 [2048, 1024], P('dp'), may hold values from -0.125 to 0.125
- out_weight: bfloat16 [1024, 1536], P('dp'), may hold values from -0.1875 to 0.1875
Outputs:
- d_queries: bfloat16 [16, 2048, 2048], P('dp', 'seq')
- d_keys: bfloat16 [16, 2048, 2048], P('dp', 'seq')
- d_values: bfloat16 [16, 2048, 2048], P('dp', 'seq')
- grad_gate: float32 [256, 2048], P('dp')
- grad_lift: float32 [2048, 1024], P('dp')
- grad_out: float32 [1024, 1536], P('dp')
Inputs may be any that keep to these rules, and one draw needn't show every extreme that they name: For each clip, feature_target is a permutation of its 2048 token positions. The 128 encoder rows of one device of seq target at most 16 tokens held by any one device of seq, and exactly 16 for some.
All inputs are finite; a program needn't handle non-finite values.
Results may differ from a plain program's by a relative error of at most 0.02.
Values may be sent and summed in bfloat16 or wider, within the bound.
A program may use at most 128 MiB of HBM per device.

v0:
```python
import math
import jax
import jax.numpy as jnp
from jax import lax
from jax.sharding import PartitionSpec as P

HD = 128
ZD = 1536
TEMB = 256
EPSILON = 1e-06


def laid_out(blocks, dim):
    blocks = jnp.moveaxis(blocks, 0, dim)
    lengths = blocks.shape
    return blocks.reshape(*lengths[:dim], lengths[dim] * lengths[dim + 1], *lengths[dim + 2 :])


def gather_packed(arrays, axis, dims):
    line = jnp.concatenate([a.reshape(-1) for a in arrays])
    lines, at, done = (lax.all_gather(line, axis), 0, [])
    for a, dim in zip(arrays, dims):
        blocks = lines[:, at : at + a.size].reshape(-1, *a.shape)
        done.append(laid_out(blocks, dim))
        at += a.size
    return tuple(done)


def embed_time(timestep):
    half_width = TEMB // 2
    frequency = jnp.exp(
        -math.log(10000.0) * jnp.arange(half_width).astype(jnp.float32) / half_width
    )
    angles = timestep.astype(jnp.float32)[:, None] * frequency[None, :]
    return jnp.concatenate([jnp.cos(angles), jnp.sin(angles)], axis=1).astype(jnp.bfloat16)


def encoder_norm(hidden, enc_gain, enc_bias):
    widened = hidden.astype(jnp.float32)
    centred = widened - jnp.mean(widened, axis=-1, keepdims=True)
    variance = jnp.mean(centred * centred, axis=-1, keepdims=True)
    return (centred * lax.rsqrt(variance + EPSILON) * enc_gain + enc_bias).astype(jnp.bfloat16)


def soft_scores(query_block, key_heads):
    scores = jnp.einsum(
        "bhd,lhd->hbl", query_block, key_heads, preferred_element_type=jnp.float32
    ) * HD ** (-0.5)
    shifted = jnp.exp(scores - jnp.max(scores, axis=-1, keepdims=True))
    return shifted / jnp.sum(shifted, axis=-1, keepdims=True)


def split_blocks(array):
    length = array.shape[0]
    block_rows = min(length, 512)
    return array.reshape(length // block_rows, block_rows, array.shape[1], array.shape[2])


def attention_forward(query_heads, key_heads, value_heads):

    def one_block(query_block):
        chances = soft_scores(query_block, key_heads).astype(jnp.bfloat16)
        return jnp.einsum(
            "hbl,lhd->bhd", chances, value_heads, preferred_element_type=jnp.float32
        ).astype(jnp.bfloat16)

    mixed = lax.map(one_block, split_blocks(query_heads))
    return mixed.reshape(query_heads.shape[0], -1)


def attention_backward(query_heads, key_heads, value_heads, grad_heads):

    def one_block(carried, pieces):
        grad_keys, grad_values = carried
        query_block, grad_block = pieces
        chances = soft_scores(query_block, key_heads)
        grad_chances = jnp.einsum(
            "bhd,lhd->hbl", grad_block, value_heads, preferred_element_type=jnp.float32
        )
        grad_values = grad_values + jnp.einsum(
            "hbl,bhd->lhd",
            chances.astype(jnp.bfloat16),
            grad_block,
            preferred_element_type=jnp.float32,
        )
        inner_sum = jnp.sum(grad_chances * chances, axis=-1, keepdims=True)
        grad_scores = (chances * (grad_chances - inner_sum) * HD ** (-0.5)).astype(jnp.bfloat16)
        grad_query = jnp.einsum(
            "hbl,lhd->bhd", grad_scores, key_heads, preferred_element_type=jnp.float32
        )
        grad_keys = grad_keys + jnp.einsum(
            "hbl,bhd->lhd", grad_scores, query_block, preferred_element_type=jnp.float32
        )
        return ((grad_keys, grad_values), grad_query.astype(jnp.bfloat16))

    zeros = jnp.zeros(key_heads.shape, jnp.float32)
    carried, grad_queries = lax.scan(
        one_block, (zeros, zeros), (split_blocks(query_heads), split_blocks(grad_heads))
    )
    length = query_heads.shape[0]
    return (
        grad_queries.reshape(length, -1),
        carried[0].reshape(length, -1).astype(jnp.bfloat16),
        carried[1].reshape(length, -1).astype(jnp.bfloat16),
    )


def shards(
    queries,
    key_states,
    value_states,
    residual,
    enc_hidden,
    enc_gain,
    enc_bias,
    feature_target,
    timestep,
    gate_weight,
    lift_weight,
    out_weight,
):
    groups = lax.axis_size("seq")
    tokens_here = queries.shape[1]
    z_width = enc_hidden.shape[2]
    capacity = 2 * tokens_here // groups
    normed = encoder_norm(enc_hidden[0], enc_gain, enc_bias)
    targets = feature_target[0]
    owning = targets // tokens_here
    onehot = (owning[:, None] == jnp.arange(groups)[None, :]).astype(jnp.int32)
    ranked = jnp.sum((jnp.cumsum(onehot, axis=0) - onehot) * onehot, axis=1)
    slotted = owning * capacity + ranked
    send_rows = jnp.zeros((groups * capacity, z_width), jnp.bfloat16).at[slotted].set(normed)
    send_places = (
        jnp.zeros((groups * capacity,), jnp.int32).at[slotted].set(targets % tokens_here + 1)
    )
    got_rows, got_places = (
        lax.all_to_all(
            send_rows.reshape(groups, capacity, z_width),
            "seq",
            split_axis=0,
            concat_axis=0,
            tiled=True,
        ),
        lax.all_to_all(
            send_places.reshape(groups, capacity), "seq", split_axis=0, concat_axis=0, tiled=True
        ),
    )
    aligned = (
        jnp.zeros((tokens_here + 1, z_width), jnp.bfloat16)
        .at[got_places.reshape(-1)]
        .set(got_rows.reshape(-1, z_width))[1:]
    )
    gate_full, lift_full, out_full = gather_packed(
        (gate_weight, lift_weight, out_weight), "dp", (0, 0, 0)
    )
    embedded = embed_time(timestep)
    gating = jnp.dot(embedded, gate_full, preferred_element_type=jnp.float32)
    query_heads, key_heads, value_heads = (
        lax.all_to_all(queries[0], "seq", split_axis=1, concat_axis=0, tiled=True),
        lax.all_to_all(key_states[0], "seq", split_axis=1, concat_axis=0, tiled=True),
        lax.all_to_all(value_states[0], "seq", split_axis=1, concat_axis=0, tiled=True),
    )
    local_width = query_heads.shape[1]

    def heads_of(array):
        return array.reshape(array.shape[0], local_width // HD, HD)

    mixed_heads = attention_forward(
        heads_of(query_heads), heads_of(key_heads), heads_of(value_heads)
    )
    mixed = lax.all_to_all(mixed_heads, "seq", split_axis=0, concat_axis=1, tiled=True)
    mixed_wide = mixed.astype(jnp.float32)
    hidden = (residual[0].astype(jnp.float32) + gating * mixed_wide).astype(jnp.bfloat16)
    lifted = jnp.dot(hidden, lift_full, preferred_element_type=jnp.float32)
    sigmoid_lift = jax.nn.sigmoid(lifted)
    activated = (lifted * sigmoid_lift).astype(jnp.bfloat16)
    predicted = jnp.dot(activated, out_full, preferred_element_type=jnp.float32)
    target_wide = aligned.astype(jnp.float32)
    pred_norm = jnp.sqrt(jnp.sum(predicted * predicted, axis=1, keepdims=True) + EPSILON)
    target_norm = jnp.sqrt(jnp.sum(target_wide * target_wide, axis=1, keepdims=True) + EPSILON)
    cosine = jnp.sum(predicted * target_wide, axis=1, keepdims=True) / (pred_norm * target_norm)
    grad_pred = (
        -1.0
        * ZD
        * (target_wide / (pred_norm * target_norm) - cosine * predicted / (pred_norm * pred_norm))
    ).astype(jnp.bfloat16)
    part_out = jnp.einsum("tp,tz->pz", activated, grad_pred, preferred_element_type=jnp.float32)
    grad_act = jnp.einsum("tz,pz->tp", grad_pred, out_full, preferred_element_type=jnp.float32)
    grad_lifted = (grad_act * sigmoid_lift * (1.0 + lifted * (1.0 - sigmoid_lift))).astype(
        jnp.bfloat16
    )
    part_lift = jnp.einsum("tf,tp->fp", hidden, grad_lifted, preferred_element_type=jnp.float32)
    grad_hidden = jnp.einsum(
        "tp,fp->tf", grad_lifted, lift_full, preferred_element_type=jnp.float32
    )
    grad_mixed = (gating * grad_hidden).astype(jnp.bfloat16)
    grad_gating = jnp.sum(grad_hidden * mixed_wide, axis=0, keepdims=True)
    part_gate = jnp.dot(
        embedded.astype(jnp.float32).T, grad_gating, precision=lax.Precision.HIGHEST
    )
    grad_heads = lax.all_to_all(grad_mixed, "seq", split_axis=1, concat_axis=0, tiled=True)
    grad_query, grad_key, grad_value = attention_backward(
        heads_of(query_heads), heads_of(key_heads), heads_of(value_heads), heads_of(grad_heads)
    )
    d_queries, d_keys, d_values = (
        lax.all_to_all(grad_query, "seq", split_axis=0, concat_axis=1, tiled=True),
        lax.all_to_all(grad_key, "seq", split_axis=0, concat_axis=1, tiled=True),
        lax.all_to_all(grad_value, "seq", split_axis=0, concat_axis=1, tiled=True),
    )
    share_gate, share_lift, share_out = (
        lax.psum_scatter(
            part_gate.astype(jnp.bfloat16), "dp", scatter_dimension=0, tiled=True
        ).astype(jnp.float32),
        lax.psum_scatter(
            part_lift.astype(jnp.bfloat16), "dp", scatter_dimension=0, tiled=True
        ).astype(jnp.float32),
        lax.psum_scatter(
            part_out.astype(jnp.bfloat16), "dp", scatter_dimension=0, tiled=True
        ).astype(jnp.float32),
    )
    grad_gate, grad_lift, grad_out = (
        lax.psum(share_gate.astype(jnp.bfloat16), "seq").astype(jnp.float32),
        lax.psum(share_lift.astype(jnp.bfloat16), "seq").astype(jnp.float32),
        lax.psum(share_out.astype(jnp.bfloat16), "seq").astype(jnp.float32),
    )
    return (d_queries[None], d_keys[None], d_values[None], grad_gate, grad_lift, grad_out)


def solution(mesh):
    in_specs = (
        P("dp", "seq", None),
        P("dp", "seq", None),
        P("dp", "seq", None),
        P("dp", "seq", None),
        P("dp", "seq", None),
        P(),
        P(),
        P("dp", "seq"),
        P("dp"),
        P("dp", None),
        P("dp", None),
        P("dp", None),
    )
    out_specs = (
        P("dp", "seq", None),
        P("dp", "seq", None),
        P("dp", "seq", None),
        P("dp", None),
        P("dp", None),
        P("dp", None),
    )
    return jax.shard_map(shards, mesh=mesh, in_specs=in_specs, out_specs=out_specs, check_vma=False)
```

profile of v0, /device:TPU:1, one launch (start us, length us, event | category | flops | bytes accessed | tf_op | source)
XLA Modules:
  0.0 702.5 jit_solution(1109292833867318314)
XLA Ops:
  13.3 12.6 %all-to-all-start = ((bf16[128,16,128]{0,2,1:T(8,128)(2,1)}), bf16[128,16,128]{0,2,1:T(8,128)(2,1)S(1)}, u32[]{:S(2)}, u32[]{:S(2)}) async-start(bf16[128,16,128]{0,2,1:T(8,128)(2,1)} %bitcast.7), calls=%async_computation | async-start | bytes 1048576 | tf_op jit(solution)/shard_map/all_to_all | solution.py:159
  26.9 20.7 %all-to-all-done = bf16[128,16,128]{0,2,1:T(8,128)(2,1)S(1)} async-done(((bf16[128,16,128]{0,2,1:T(8,128)(2,1)}), bf16[128,16,128]{0,2,1:T(8,128)(2,1)S(1)}, u32[]{:S(2)}, u32[]{:S(2)}) %all-to-all-start) | async-done | bytes 524320 | tf_op jit(solution)/shard_map/all_to_all | solution.py:159
  47.6 4.5 all-to-all-start.1
  53.1 17.1 %all-to-all-done.1 = bf16[128,16,128]{0,2,1:T(8,128)(2,1)S(1)} async-done(((bf16[128,16,128]{0,2,1:T(8,128)(2,1)}), bf16[128,16,128]{0,2,1:T(8,128)(2,1)S(1)}, u32[]{:S(2)}, u32[]{:S(2)}) %all-to-all-start.1) | async-done | bytes 524320 | tf_op jit(solution)/shard_map/all_to_all | solution.py:160
  70.2 5.5 all-to-all-start.4
  78.3 20.8 %all-to-all-done.4 = bf16[128,16,128]{0,2,1:T(8,128)(2,1)S(1)} async-done(((bf16[128,16,128]{0,2,1:T(8,128)(2,1)}), bf16[128,16,128]{0,2,1:T(8,128)(2,1)S(1)}, u32[]{:S(2)}, u32[]{:S(2)}) %all-to-all-start.4) | async-done | bytes 524320 | tf_op jit(solution)/shard_map/all_to_all | solution.py:161
  106.7 6.0 all-to-all-done.2
  117.7 13.1 %while.25 = (s32[]{:T(128)}, bf16[4,512,1,128]{3,1,2,0:T(8,128)(2,1)}, bf16[4,512,1,128]{3,1,2,0:T(8,128)(2,1)S(1)}, bf16[2048,1,128]{2,0,1:T(8,128)(2,1)S(1)}, bf16[2048,1,128]{2,0,1:T(8,128)(2,1)S(1)}, /*index=5*/s32[]{:T(128)}) while((s32[]{:T(128)}, bf16[4,512,1,128]{3,1,2,0:T(8,128)(2,1)}, bf16[4,512,1,128]{3,1,2,0:T(8,128)(2,1)S(1)}, ...), condition=%wide.region_10.11_spmd, body=%wide.region_7.10_spmd.sunk | while | flops 546372608 | bytes 13904457 | solution.py:67
  130.8 11.7 %all-to-all-done.3 = bf16[16,16,1536]{2,1,0:T(8,128)(2,1)S(1)} async-done(((bf16[16,16,1536]{2,1,0:T(8,128)(2,1)}), bf16[16,16,1536]{2,1,0:T(8,128)(2,1)S(1)}, u32[]{:S(2)}, u32[]{:S(2)}) %all-to-all-start.3) | async-done | bytes 786464 | tf_op jit(solution)/shard_map/all_to_all | solution.py:137
  142.5 4.9 all-to-all-start.5
  152.0 15.6 %all-to-all-done.5 = bf16[16,128,128]{2,1,0:T(8,128)(2,1)} async-done(((bf16[16,128,128]{2,1,0:T(8,128)(2,1)}), bf16[16,128,128]{2,1,0:T(8,128)(2,1)}, u32[]{:S(2)}, u32[]{:S(2)}) %all-to-all-start.5) | async-done | bytes 524320 | tf_op jit(solution)/shard_map/all_to_all | solution.py:171
  172.9 7.7 %reshape.446 = bf16[16,262144]{1,0:T(8,128)(2,1)} reshape(bf16[4194304]{0:T(1024)(128)(2,1)} %all-gather.3.cloned.1.call-done) | data formatting | bytes 16777216 | tf_op jit(solution)/shard_map/all_gather | solution.py:21
  180.5 4.7 slice.18
  189.9 4.8 reshape_reshape.18
  214.9 4.8 all-to-all-start.6
  224.2 9.3 %all-to-all-done.6 = bf16[128,16,128]{2,0,1:T(8,128)(2,1)} async-done(((bf16[128,16,128]{2,0,1:T(8,128)(2,1)}), bf16[128,16,128]{2,0,1:T(8,128)(2,1)}, u32[]{:S(2)}, u32[]{:S(2)}) %all-to-all-start.6) | async-done | bytes 524320 | tf_op jit(solution)/shard_map/all_to_all | solution.py:201
  234.4 51.8 %while.26 = (s32[]{:T(128)}, f32[2048,1,128]{0,2,1:T(8,128)S(1)}, f32[2048,1,128]{0,2,1:T(8,128)S(1)}, bf16[4,512,1,128]{3,1,2,0:T(8,128)(2,1)}, bf16[4,512,1,12...) while((s32[]{:T(128)}, f32[2048,1,128]{0,2,1:T(8,128)S(1)}, ...), condition=%wide.region_18.19_spmd.clone, body=%wide.region_14.18_spmd.clone.sunk | while | flops 1365309952 | bytes 77749960 | solution.py:97
  287.3 4.5 all-to-all-start.8
  292.1 14.2 %all-to-all-done.8 = bf16[16,128,128]{2,1,0:T(8,128)(2,1)S(1)} async-done(((bf16[16,128,128]{2,1,0:T(8,128)(2,1)}), bf16[16,128,128]{2,1,0:T(8,128)(2,1)S(1)}, u32[]{:S(2)}, u32[]{:S(2)}) %all-to-all-start.8) | async-done | bytes 524320 | tf_op jit(solution)/shard_map/all_to_all | solution.py:207
  306.3 17.9 %all_to_all.133 = bf16[16,128,128]{2,1,0:T(8,128)(2,1)S(1)} all-to-all(bf16[16,128,128]{2,1,0:T(8,128)(2,1)S(1)} %bitcast.232), channel_id=1, replica_groups=mesh['dp'=16,'seq'=16] {'seq'}, dimensions={0} | all-to-all | bytes 1048576 | tf_op jit(solution)/shard_map/all_to_all | solution.py:208
  324.2 4.5 all-to-all-start.7
  328.8 82.0 %reduce-scatter.8.cloned.1.call-done = bf16[64,1536]{1,0:T(8,128)(2,1)} async-done(((bf16[1024,1536]{1,0:T(8,128)(2,1)}), bf16[64,1536]{1,0:T(8,128)(2,1)}) %reduce-scatter.8.cloned.1.call-update) | async-done | bytes 196624 | tf_op jit(solution)/shard_map/reduce_scatter | solution.py:217
  410.8 92.8 %reduce-scatter.6.cloned.1.call-done = bf16[128,1024]{1,0:T(8,128)(2,1)} async-done(((bf16[2048,1024]{1,0:T(8,128)(2,1)}), bf16[128,1024]{1,0:T(8,128)(2,1)}) %reduce-scatter.6.cloned.1.call-update) | async-done | bytes 262160 | tf_op jit(solution)/shard_map/reduce_scatter | solution.py:214
  507.6 183.5 %all-reduce.3.cloned.1.call-done = (bf16[16,2048]{1,0:T(8,128)(2,1)}, bf16[128,1024]{1,0:T(8,128)(2,1)}, bf16[64,1536]{1,0:T(8,128)(2,1)}) async-done(((bf16[16,2048]{1,0:T(8,128)(2,1)}, bf16[128,1024]{1,0:T(8,128)(2,1)}, bf16[64,1536]{1,0:T(8,128)(2,1)}), (bf16[16,2048]{1,0:T(8,128)(2,1)}, bf16[128,1024]{1,0:T(8,128)(2,1)}, bf16[64,1536]{1,0:T(8,128)(2,1)})) %all-reduce.3.cloned.1.call-update) | async-done | bytes 524304 | tf_op jit(solution)/shard_map/psum | solution.py:222
  (172 shorter events, 137.4 us)
Async XLA Ops:
  7.2 18.8 %copy-start.8 = (bf16[1,128,2048]{2,1,0:T(8,128)(2,1)S(1)}, bf16[1,128,2048]{2,1,0:T(8,128)(2,1)}, u32[]{:S(2)}) copy-start(bf16[1,128,2048]{2,1,0:T(8,128)(2,1)} %param.17) | copy-start | bytes 1572868
  7.2 44.9 %copy-start.9 = (bf16[1,128,2048]{2,1,0:T(8,128)(2,1)S(1)}, bf16[1,128,2048]{2,1,0:T(8,128)(2,1)}, u32[]{:S(2)}) copy-start(bf16[1,128,2048]{2,1,0:T(8,128)(2,1)} %param.18) | copy-start | bytes 1572868
  7.2 45.9 %copy-start.15 = (s32[1,128]{1,0:T(1,128)S(1)}, s32[1,128]{1,0:T(1,128)}, u32[]{:S(2)}) copy-start(s32[1,128]{1,0:T(1,128)} %param.23) | copy-start | bytes 1540
  7.2 165.7 %all-gather.3.cloned.1.call-start = ((), (), s32[]{:S(2)}) async-start(), calls=%async_computation.16 | async-start | bytes 8912896 | tf_op jit(solution)/shard_map/all_gather | solution.py:21
  9.5 68.4 %copy-start.5 = (bf16[1,128,1536]{2,1,0:T(8,128)(2,1)S(1)}, bf16[1,128,1536]{2,1,0:T(8,128)(2,1)}, u32[]{:S(2)}) copy-start(bf16[1,128,1536]{2,1,0:T(8,128)(2,1)} %param.20) | copy-start | bytes 1179652
  11.2 92.2 %copy-start.13 = (f32[1536]{0:T(1024)S(1)}, f32[1536]{0:T(1024)}, u32[]{:S(2)}) copy-start(f32[1536]{0:T(1024)} %param.22) | copy-start | bytes 18436
  11.2 92.2 %copy-start.14 = (f32[1536]{0:T(1024)S(1)}, f32[1536]{0:T(1024)}, u32[]{:S(2)}) copy-start(f32[1536]{0:T(1024)} %param.21) | copy-start | bytes 18436
  13.3 34.3 %all-to-all-start = ((bf16[128,16,128]{0,2,1:T(8,128)(2,1)}), bf16[128,16,128]{0,2,1:T(8,128)(2,1)S(1)}, u32[]{:S(2)}, u32[]{:S(2)}) async-start(bf16[128,16,128]{0,2,1:T(8,128)(2,1)} %bitcast.7), calls=%async_computation | async-start | bytes 1048576 | tf_op jit(solution)/shard_map/all_to_all | solution.py:159
  47.6 22.6 %all-to-all-start.1 = ((bf16[128,16,128]{0,2,1:T(8,128)(2,1)}), bf16[128,16,128]{0,2,1:T(8,128)(2,1)S(1)}, u32[]{:S(2)}, u32[]{:S(2)}) async-start(bf16[128,16,128]{0,2,1:T(8,128)(2,1)} %bitcast.11), calls=%async_computation.1 | async-start | bytes 1048576 | tf_op jit(solution)/shard_map/all_to_all | solution.py:160
  70.2 28.9 %all-to-all-start.4 = ((bf16[128,16,128]{0,2,1:T(8,128)(2,1)}), bf16[128,16,128]{0,2,1:T(8,128)(2,1)S(1)}, u32[]{:S(2)}, u32[]{:S(2)}) async-start(bf16[128,16,128]{0,2,1:T(8,128)(2,1)} %bitcast.25), calls=%async_computation.4 | async-start | bytes 1048576 | tf_op jit(solution)/shard_map/all_to_all | solution.py:161
  99.1 13.6 %all-to-all-start.2 = ((s32[16,1,16]{2,1,0:T(1,128)}), s32[16,1,16]{2,1,0:T(1,128)S(1)}, u32[]{:S(2)}, u32[]{:S(2)}) async-start(s32[16,1,16]{2,1,0:T(1,128)} %all_to_all.105), calls=%async_computation.2 | async-start | bytes 16384 | tf_op jit(solution)/shard_map/all_to_all | solution.py:144
  112.8 29.7 %all-to-all-start.3 = ((bf16[16,16,1536]{2,1,0:T(8,128)(2,1)}), bf16[16,16,1536]{2,1,0:T(8,128)(2,1)S(1)}, u32[]{:S(2)}, u32[]{:S(2)}) async-start(bf16[16,16,1536]{2,1,0:T(8,128)(2,1)} %bitcast.22), calls=%async_computation.3 | async-start | bytes 1572864 | tf_op jit(solution)/shard_map/all_to_all | solution.py:137
  130.8 21.2 %copy-start.10 = (bf16[2048,1,128]{2,0,1:T(8,128)(2,1)}, bf16[2048,1,128]{2,0,1:T(8,128)(2,1)S(1)}, u32[]{:S(2)}) copy-start(bf16[2048,1,128]{2,0,1:T(8,128)(2,1)S(1)} %get-tuple-element.385) | copy-start | bytes 1572868
  142.5 25.0 %all-to-all-start.5 = ((bf16[16,128,128]{2,1,0:T(8,128)(2,1)}), bf16[16,128,128]{2,1,0:T(8,128)(2,1)}, u32[]{:S(2)}, u32[]{:S(2)}) async-start(bf16[16,128,128]{2,1,0:T(8,128)(2,1)} %bitcast.28), calls=%async_computation.5 | async-start | bytes 1048576 | tf_op jit(solution)/shard_map/all_to_all | solution.py:171
  147.5 181.4 %reduce-scatter.4.cloned.1.call-start = ((), (), s32[]{:S(2)}) async-start(), calls=%async_computation.13 | async-start | bytes 1114112 | tf_op jit(solution)/shard_map/reduce_scatter | solution.py:211
  180.5 6.2 copy-start.3
  194.7 5.7 copy-start.4
  209.7 201.1 %reduce-scatter.8.cloned.1.call-start = ((), (), s32[]{:S(2)}) async-start(), calls=%async_computation.15 | async-start | bytes 3342336 | tf_op jit(solution)/shard_map/reduce_scatter | solution.py:217
  214.9 18.6 %all-to-all-start.6 = ((bf16[128,16,128]{2,0,1:T(8,128)(2,1)}), bf16[128,16,128]{2,0,1:T(8,128)(2,1)}, u32[]{:S(2)}, u32[]{:S(2)}) async-start(bf16[128,16,128]{2,0,1:T(8,128)(2,1)} %bitcast.194), calls=%async_computation.6 | async-start | bytes 1048576 | tf_op jit(solution)/shard_map/all_to_all | solution.py:201
  219.6 284.0 %reduce-scatter.6.cloned.1.call-start = ((), (), s32[]{:S(2)}) async-start(), calls=%async_computation.14 | async-start | bytes 4456448 | tf_op jit(solution)/shard_map/reduce_scatter | solution.py:214
  224.2 10.2 %copy-start.7 = (f32[2048,1,128]{0,2,1:T(8,128)S(1)}, f32[2048,1,128]{0,2,1:T(8,128)}, u32[]{:S(2)}) copy-start(f32[2048,1,128]{0,2,1:T(8,128)} %custom-call.1) | copy-start | bytes 3145732
  287.3 19.0 %all-to-all-start.8 = ((bf16[16,128,128]{2,1,0:T(8,128)(2,1)}), bf16[16,128,128]{2,1,0:T(8,128)(2,1)S(1)}, u32[]{:S(2)}, u32[]{:S(2)}) async-start(bf16[16,128,128]{2,1,0:T(8,128)(2,1)} %bitcast.37), calls=%async_computation.8 | async-start | bytes 1048576 | tf_op jit(solution)/shard_map/all_to_all | solution.py:207
  324.2 182.0 %all-to-all-start.7 = ((bf16[16,128,128]{2,1,0:T(8,128)(2,1)}), bf16[16,128,128]{2,1,0:T(8,128)(2,1)S(1)}, u32[]{:S(2)}, u32[]{:S(2)}) async-start(bf16[16,128,128]{2,1,0:T(8,128)(2,1)} %bitcast.34), calls=%async_computation.7 | async-start | bytes 1048576 | tf_op jit(solution)/shard_map/all_to_all | solution.py:206
  328.8 362.3 %all-reduce.3.cloned.1.call-start = ((), (), s32[]{:S(2)}) async-start(), calls=%async_computation.17 | async-start | bytes 1048576 | tf_op jit(solution)/shard_map/psum | solution.py:222
  (17 other events, 52.7 us)
Sparse Core Ops, SparseCore 0:
  11.4 155.1 all-gather.2
  209.8 102.7 reduce-scatter.3
  315.3 95.4 reduce-scatter.7
  413.4 90.2 reduce-scatter.5
  506.6 184.4 all-reduce.2
where the time goes:
time: 704 us; the launch traced here: 703 us
  waiting for transfers between devices  474 us (67%)
  matrix products  61 us (9%)
  local copies, waits for them, and re-layouts  59.7 us (8%)
  starting transfers between devices  50.1 us (7%)
  other arithmetic  25 us (4%)
  blocking collectives  17.9 us (3%)
  between operations  14.7 us (2%)
    psum x1, waiting for transfers between devices, shards(): lax.psum(share_gate.astype(jnp.bfloat16), 'seq').astype(jnp.float32)  183 us
    reduce_scatter x1, waiting for transfers between devices, shards(): lax.psum_scatter(part_lift.astype(jnp.bfloat16), 'dp', scatter_dimension=...  92.8 us
    reduce_scatter x1, waiting for transfers between devices, shards(): lax.psum_scatter(part_out.astype(jnp.bfloat16), 'dp', scatter_dimension=0...  82 us
    all_to_all x1, waiting for transfers between devices, shards(): lax.all_to_all(value_states[0], 'seq', split_axis=1, concat_axis=0, tiled...  20.8 us
    all_to_all x1, waiting for transfers between devices, shards(): lax.all_to_all(queries[0], 'seq', split_axis=1, concat_axis=0, tiled=True)  20.7 us
    all_to_all x1, blocking collectives, shards(): lax.all_to_all(grad_value, 'seq', split_axis=0, concat_axis=1, tiled=True)  17.9 us
    all_to_all x1, waiting for transfers between devices, shards(): lax.all_to_all(key_states[0], 'seq', split_axis=1, concat_axis=0, tiled=T...  17.1 us
    all_to_all x1, waiting for transfers between devices, shards(): lax.all_to_all(mixed_heads, 'seq', split_axis=0, concat_axis=1, tiled=True)  15.6 us
  transfers between devices with their start and end apart: 14, of which 11 were waited for; matrix products, arithmetic and copies ran while one was open for 13% of the time, Pallas kernels for 0%

commit v1 on v0

--- a/solution.py
+++ b/solution.py
@@ -219,7 +219,7 @@
         ).astype(jnp.float32),
     )
     grad_gate, grad_lift, grad_out = (
-        lax.psum(share_gate.astype(jnp.bfloat16), "seq").astype(jnp.float32),
+        jnp.sum(jax.lax.all_gather(share_gate.astype(jnp.bfloat16), "seq"), 0).astype(jnp.float32),
         lax.psum(share_lift.astype(jnp.bfloat16), "seq").astype(jnp.float32),
         lax.psum(share_out.astype(jnp.bfloat16), "seq").astype(jnp.float32),
     )

time: 704 us -> 755 us (1.072)
  waiting for transfers between devices: 474 us -> 504 us
  blocking collectives: 17.9 us -> 32.1 us
    all_gather x0 -> x1, waiting for transfers between devices: none -> 62.1 us  [shards(): jax.lax.all_gather(share_gate.astype(jnp.bfloat16), 'seq')]
    reduce_scatter x1, waiting for transfers between devices: 82 us -> 58.2 us  [shards(): lax.psum_scatter(part_out.astype(jnp.bfloat16), 'dp', scatter_dimension=0...]
    reduce_scatter x1, waiting for transfers between devices: 0.02 us -> 20.8 us  [shards(): lax.psum_scatter(part_gate.astype(jnp.bfloat16), 'dp', scatter_dimension=...]
    all_to_all x1, waiting for transfers between devices: 14.2 us -> 0.01 us  [shards(): lax.all_to_all(grad_key, 'seq', split_axis=0, concat_axis=1, tiled=True)]
    all_to_all x1, blocking collectives: 17.9 us -> 32.1 us  [shards(): lax.all_to_all(grad_value, 'seq', split_axis=0, concat_axis=1, tiled=True)]
    psum x1, waiting for transfers between devices: 183 us -> 170 us  [shards(): lax.psum(share_lift.astype(jnp.bfloat16), 'seq').astype(jnp.float32)]
  transfers between devices with their start and end apart: 14 -> 15, of which waited for: 11 -> 12; matrix products, arithmetic and copies ran while one was open for 13% -> 12% of each run, Pallas kernels for 0% -> 0%
where the time goes in v1:
time: 755 us; the launch traced here: 752 us
  waiting for transfers between devices  504 us (67%)
  matrix products  61 us (8%)
  local copies, waits for them, and re-layouts  59.7 us (8%)
  starting transfers between devices  55.1 us (7%)
  blocking collectives  32.1 us (4%)
  other arithmetic  25.6 us (3%)
  between operations  15.1 us (2%)
    psum x1, waiting for transfers between devices, shards(): lax.psum(share_lift.astype(jnp.bfloat16), 'seq').astype(jnp.float32)  170 us
    reduce_scatter x1, waiting for transfers between devices, shards(): lax.psum_scatter(part_lift.astype(jnp.bfloat16), 'dp', scatter_dimension=...  91.3 us
    all_gather x1, waiting for transfers between devices, shards(): jax.lax.all_gather(share_gate.astype(jnp.bfloat16), 'seq')  62.1 us
    reduce_scatter x1, waiting for transfers between devices, shards(): lax.psum_scatter(part_out.astype(jnp.bfloat16), 'dp', scatter_dimension=0...  58.2 us
    all_to_all x1, blocking collectives, shards(): lax.all_to_all(grad_value, 'seq', split_axis=0, concat_axis=1, tiled=True)  32.1 us
    all_to_all x1, waiting for transfers between devices, shards(): lax.all_to_all(value_states[0], 'seq', split_axis=1, concat_axis=0, tiled...  20.8 us
    reduce_scatter x1, waiting for transfers between devices, shards(): lax.psum_scatter(part_gate.astype(jnp.bfloat16), 'dp', scatter_dimension=...  20.8 us
    all_to_all x1, waiting for transfers between devices, shards(): lax.all_to_all(queries[0], 'seq', split_axis=1, concat_axis=0, tiled=True)  20.7 us
  transfers between devices with their start and end apart: 15, of which 12 were waited for; matrix products, arithmetic and copies ran while one was open for 12% of the time, Pallas kernels for 0%

profile of v1, /device:TPU:1, one launch (start us, length us, event | category | flops | bytes accessed | tf_op | source)
XLA Modules:
  0.0 752.5 jit_solution(14621622369834452405)
XLA Ops:
  13.3 12.6 %all-to-all-start = ((bf16[128,16,128]{0,2,1:T(8,128)(2,1)}), bf16[128,16,128]{0,2,1:T(8,128)(2,1)S(1)}, u32[]{:S(2)}, u32[]{:S(2)}) async-start(bf16[128,16,128]{0,2,1:T(8,128)(2,1)} %bitcast.7), calls=%async_computation | async-start | bytes 1048576 | tf_op jit(solution)/shard_map/all_to_all | solution.py:159
  26.9 20.7 %all-to-all-done = bf16[128,16,128]{0,2,1:T(8,128)(2,1)S(1)} async-done(((bf16[128,16,128]{0,2,1:T(8,128)(2,1)}), bf16[128,16,128]{0,2,1:T(8,128)(2,1)S(1)}, u32[]{:S(2)}, u32[]{:S(2)}) %all-to-all-start) | async-done | bytes 524320 | tf_op jit(solution)/shard_map/all_to_all | solution.py:159
  53.1 17.1 %all-to-all-done.1 = bf16[128,16,128]{0,2,1:T(8,128)(2,1)S(1)} async-done(((bf16[128,16,128]{0,2,1:T(8,128)(2,1)}), bf16[128,16,128]{0,2,1:T(8,128)(2,1)S(1)}, u32[]{:S(2)}, u32[]{:S(2)}) %all-to-all-start.1) | async-done | bytes 524320 | tf_op jit(solution)/shard_map/all_to_all | solution.py:160
  70.2 5.5 all-to-all-start.4
  78.3 20.8 %all-to-all-done.4 = bf16[128,16,128]{0,2,1:T(8,128)(2,1)S(1)} async-done(((bf16[128,16,128]{0,2,1:T(8,128)(2,1)}), bf16[128,16,128]{0,2,1:T(8,128)(2,1)S(1)}, u32[]{:S(2)}, u32[]{:S(2)}) %all-to-all-start.4) | async-done | bytes 524320 | tf_op jit(solution)/shard_map/all_to_all | solution.py:161
  106.7 6.0 all-to-all-done.2
  117.7 13.1 %while.25 = (s32[]{:T(128)}, bf16[4,512,1,128]{3,1,2,0:T(8,128)(2,1)}, bf16[4,512,1,128]{3,1,2,0:T(8,128)(2,1)S(1)}, bf16[2048,1,128]{2,0,1:T(8,128)(2,1)S(1)}, bf16[2048,1,128]{2,0,1:T(8,128)(2,1)S(1)}, /*index=5*/s32[]{:T(128)}) while((s32[]{:T(128)}, bf16[4,512,1,128]{3,1,2,0:T(8,128)(2,1)}, bf16[4,512,1,128]{3,1,2,0:T(8,128)(2,1)S(1)}, ...), condition=%wide.region_10.11_spmd, body=%wide.region_7.10_spmd.sunk | while | flops 546372608 | bytes 13904457 | solution.py:67
  130.8 11.7 %all-to-all-done.3 = bf16[16,16,1536]{2,1,0:T(8,128)(2,1)S(1)} async-done(((bf16[16,16,1536]{2,1,0:T(8,128)(2,1)}), bf16[16,16,1536]{2,1,0:T(8,128)(2,1)S(1)}, u32[]{:S(2)}, u32[]{:S(2)}) %all-to-all-start.3) | async-done | bytes 786464 | tf_op jit(solution)/shard_map/all_to_all | solution.py:137
  142.5 4.9 all-to-all-start.5
  152.0 15.6 %all-to-all-done.5 = bf16[16,128,128]{2,1,0:T(8,128)(2,1)} async-done(((bf16[16,128,128]{2,1,0:T(8,128)(2,1)}), bf16[16,128,128]{2,1,0:T(8,128)(2,1)}, u32[]{:S(2)}, u32[]{:S(2)}) %all-to-all-start.5) | async-done | bytes 524320 | tf_op jit(solution)/shard_map/all_to_all | solution.py:171
  172.9 7.7 %reshape.446 = bf16[16,262144]{1,0:T(8,128)(2,1)} reshape(bf16[4194304]{0:T(1024)(128)(2,1)} %all-gather.5.cloned.1.call-done) | data formatting | bytes 16777216 | tf_op jit(solution)/shard_map/all_gather | solution.py:21
  180.5 4.7 slice.18
  189.9 4.8 reshape_reshape.18
  214.9 4.8 all-to-all-start.6
  224.2 9.3 %all-to-all-done.6 = bf16[128,16,128]{2,0,1:T(8,128)(2,1)} async-done(((bf16[128,16,128]{2,0,1:T(8,128)(2,1)}), bf16[128,16,128]{2,0,1:T(8,128)(2,1)}, u32[]{:S(2)}, u32[]{:S(2)}) %all-to-all-start.6) | async-done | bytes 524320 | tf_op jit(solution)/shard_map/all_to_all | solution.py:201
  234.4 51.8 %while.26 = (s32[]{:T(128)}, f32[2048,1,128]{0,2,1:T(8,128)S(1)}, f32[2048,1,128]{0,2,1:T(8,128)S(1)}, bf16[4,512,1,128]{3,1,2,0:T(8,128)(2,1)}, bf16[4,512,1,12...) while((s32[]{:T(128)}, f32[2048,1,128]{0,2,1:T(8,128)S(1)}, ...), condition=%wide.region_18.19_spmd.clone, body=%wide.region_14.18_spmd.clone.sunk | while | flops 1365309952 | bytes 77749960 | solution.py:97
  287.3 4.5 all-to-all-start.8
  291.8 20.8 %reduce-scatter.4.cloned.1.call-done = bf16[16,2048]{1,0:T(8,128)(2,1)} async-done(((bf16[256,2048]{1,0:T(8,128)(2,1)}), bf16[16,2048]{1,0:T(8,128)(2,1)}) %reduce-scatter.4.cloned.1.call-update) | async-done | bytes 65552 | tf_op jit(solution)/shard_map/reduce_scatter | solution.py:211
  313.0 32.1 %all_to_all.133 = bf16[16,128,128]{2,1,0:T(8,128)(2,1)S(1)} all-to-all(bf16[16,128,128]{2,1,0:T(8,128)(2,1)S(1)} %bitcast.233), channel_id=1, replica_groups=mesh['dp'=16,'seq'=16] {'seq'}, dimensions={0} | all-to-all | bytes 1048576 | tf_op jit(solution)/shard_map/all_to_all | solution.py:208
  345.0 9.5 %all-to-all-start.7 = ((bf16[16,128,128]{2,1,0:T(8,128)(2,1)}), bf16[16,128,128]{2,1,0:T(8,128)(2,1)S(1)}, u32[]{:S(2)}, u32[]{:S(2)}) async-start(bf16[16,128,128]{2,1,0:T(8,128)(2,1)} %bitcast.34), calls=%async_computation.7 | async-start | bytes 1048576 | tf_op jit(solution)/shard_map/all_to_all | solution.py:206
  354.6 58.2 %reduce-scatter.8.cloned.1.call-done = bf16[64,1536]{1,0:T(8,128)(2,1)} async-done(((bf16[1024,1536]{1,0:T(8,128)(2,1)}), bf16[64,1536]{1,0:T(8,128)(2,1)}) %reduce-scatter.8.cloned.1.call-update) | async-done | bytes 196624 | tf_op jit(solution)/shard_map/reduce_scatter | solution.py:217
  412.8 91.3 %reduce-scatter.6.cloned.1.call-done = bf16[128,1024]{1,0:T(8,128)(2,1)} async-done(((bf16[2048,1024]{1,0:T(8,128)(2,1)}), bf16[128,1024]{1,0:T(8,128)(2,1)}) %reduce-scatter.6.cloned.1.call-update) | async-done | bytes 262160 | tf_op jit(solution)/shard_map/reduce_scatter | solution.py:214
  508.0 62.1 %all-gather.7.cloned.1.call-done = bf16[256,2048]{1,0:T(8,128)(2,1)} async-done(((bf16[16,2048]{1,0:T(8,128)(2,1)}), bf16[256,2048]{1,0:T(8,128)(2,1)}) %all-gather.7.cloned.1.call-update) | async-done | bytes 1048592 | tf_op jit(solution)/shard_map/all_gather | solution.py:222
  572.2 169.9 %all-reduce.3.cloned.1.call-done = (bf16[128,1024]{1,0:T(8,128)(2,1)}, bf16[64,1536]{1,0:T(8,128)(2,1)}) async-done(((bf16[128,1024]{1,0:T(8,128)(2,1)}, bf16[64,1536]{1,0:T(8,128)(2,1)}), (bf16[128,1024]{1,0:T(8,128)(2,1)}, bf16[64,1536]{1,0:T(8,128)(2,1)})) %all-reduce.3.cloned.1.call-update) | async-done | bytes 458768 | tf_op jit(solution)/shard_map/psum | solution.py:223
  (176 shorter events, 142.4 us)
Async XLA Ops:
  7.2 18.8 %copy-start.8 = (bf16[1,128,2048]{2,1,0:T(8,128)(2,1)S(1)}, bf16[1,128,2048]{2,1,0:T(8,128)(2,1)}, u32[]{:S(2)}) copy-start(bf16[1,128,2048]{2,1,0:T(8,128)(2,1)} %param.17) | copy-start | bytes 1572868
  7.2 44.9 %copy-start.9 = (bf16[1,128,2048]{2,1,0:T(8,128)(2,1)S(1)}, bf16[1,128,2048]{2,1,0:T(8,128)(2,1)}, u32[]{:S(2)}) copy-start(bf16[1,128,2048]{2,1,0:T(8,128)(2,1)} %param.18) | copy-start | bytes 1572868
  7.2 45.9 %copy-start.15 = (s32[1,128]{1,0:T(1,128)S(1)}, s32[1,128]{1,0:T(1,128)}, u32[]{:S(2)}) copy-start(s32[1,128]{1,0:T(1,128)} %param.23) | copy-start | bytes 1540
  7.2 165.7 %all-gather.5.cloned.1.call-start = ((), (), s32[]{:S(2)}) async-start(), calls=%async_computation.16 | async-start | bytes 8912896 | tf_op jit(solution)/shard_map/all_gather | solution.py:21
  9.5 68.4 %copy-start.5 = (bf16[1,128,1536]{2,1,0:T(8,128)(2,1)S(1)}, bf16[1,128,1536]{2,1,0:T(8,128)(2,1)}, u32[]{:S(2)}) copy-start(bf16[1,128,1536]{2,1,0:T(8,128)(2,1)} %param.20) | copy-start | bytes 1179652
  11.2 92.2 %copy-start.13 = (f32[1536]{0:T(1024)S(1)}, f32[1536]{0:T(1024)}, u32[]{:S(2)}) copy-start(f32[1536]{0:T(1024)} %param.22) | copy-start | bytes 18436
  11.2 92.2 %copy-start.14 = (f32[1536]{0:T(1024)S(1)}, f32[1536]{0:T(1024)}, u32[]{:S(2)}) copy-start(f32[1536]{0:T(1024)} %param.21) | copy-start | bytes 18436
  13.3 34.3 %all-to-all-start = ((bf16[128,16,128]{0,2,1:T(8,128)(2,1)}), bf16[128,16,128]{0,2,1:T(8,128)(2,1)S(1)}, u32[]{:S(2)}, u32[]{:S(2)}) async-start(bf16[128,16,128]{0,2,1:T(8,128)(2,1)} %bitcast.7), calls=%async_computation | async-start | bytes 1048576 | tf_op jit(solution)/shard_map/all_to_all | solution.py:159
  47.6 22.6 %all-to-all-start.1 = ((bf16[128,16,128]{0,2,1:T(8,128)(2,1)}), bf16[128,16,128]{0,2,1:T(8,128)(2,1)S(1)}, u32[]{:S(2)}, u32[]{:S(2)}) async-start(bf16[128,16,128]{0,2,1:T(8,128)(2,1)} %bitcast.11), calls=%async_computation.1 | async-start | bytes 1048576 | tf_op jit(solution)/shard_map/all_to_all | solution.py:160
  70.2 28.9 %all-to-all-start.4 = ((bf16[128,16,128]{0,2,1:T(8,128)(2,1)}), bf16[128,16,128]{0,2,1:T(8,128)(2,1)S(1)}, u32[]{:S(2)}, u32[]{:S(2)}) async-start(bf16[128,16,128]{0,2,1:T(8,128)(2,1)} %bitcast.25), calls=%async_computation.4 | async-start | bytes 1048576 | tf_op jit(solution)/shard_map/all_to_all | solution.py:161
  99.1 13.6 %all-to-all-start.2 = ((s32[16,1,16]{2,1,0:T(1,128)}), s32[16,1,16]{2,1,0:T(1,128)S(1)}, u32[]{:S(2)}, u32[]{:S(2)}) async-start(s32[16,1,16]{2,1,0:T(1,128)} %all_to_all.105), calls=%async_computation.2 | async-start | bytes 16384 | tf_op jit(solution)/shard_map/all_to_all | solution.py:144
  112.8 29.7 %all-to-all-start.3 = ((bf16[16,16,1536]{2,1,0:T(8,128)(2,1)}), bf16[16,16,1536]{2,1,0:T(8,128)(2,1)S(1)}, u32[]{:S(2)}, u32[]{:S(2)}) async-start(bf16[16,16,1536]{2,1,0:T(8,128)(2,1)} %bitcast.22), calls=%async_computation.3 | async-start | bytes 1572864 | tf_op jit(solution)/shard_map/all_to_all | solution.py:137
  130.8 21.2 %copy-start.10 = (bf16[2048,1,128]{2,0,1:T(8,128)(2,1)}, bf16[2048,1,128]{2,0,1:T(8,128)(2,1)S(1)}, u32[]{:S(2)}) copy-start(bf16[2048,1,128]{2,0,1:T(8,128)(2,1)S(1)} %get-tuple-element.403) | copy-start | bytes 1572868
  142.5 25.0 %all-to-all-start.5 = ((bf16[16,128,128]{2,1,0:T(8,128)(2,1)}), bf16[16,128,128]{2,1,0:T(8,128)(2,1)}, u32[]{:S(2)}, u32[]{:S(2)}) async-start(bf16[16,128,128]{2,1,0:T(8,128)(2,1)} %bitcast.28), calls=%async_computation.5 | async-start | bytes 1048576 | tf_op jit(solution)/shard_map/all_to_all | solution.py:171
  147.5 165.1 %reduce-scatter.4.cloned.1.call-start = ((), (), s32[]{:S(2)}) async-start(), calls=%async_computation.13 | async-start | bytes 1114112 | tf_op jit(solution)/shard_map/reduce_scatter | solution.py:211
  180.5 6.2 copy-start.3
  209.7 203.1 %reduce-scatter.8.cloned.1.call-start = ((), (), s32[]{:S(2)}) async-start(), calls=%async_computation.15 | async-start | bytes 3342336 | tf_op jit(solution)/shard_map/reduce_scatter | solution.py:217
  214.9 18.6 %all-to-all-start.6 = ((bf16[128,16,128]{2,0,1:T(8,128)(2,1)}), bf16[128,16,128]{2,0,1:T(8,128)(2,1)}, u32[]{:S(2)}, u32[]{:S(2)}) async-start(bf16[128,16,128]{2,0,1:T(8,128)(2,1)} %bitcast.195), calls=%async_computation.6 | async-start | bytes 1048576 | tf_op jit(solution)/shard_map/all_to_all | solution.py:201
  219.6 284.5 %reduce-scatter.6.cloned.1.call-start = ((), (), s32[]{:S(2)}) async-start(), calls=%async_computation.14 | async-start | bytes 4456448 | tf_op jit(solution)/shard_map/reduce_scatter | solution.py:214
  224.2 10.2 %copy-start.7 = (f32[2048,1,128]{0,2,1:T(8,128)S(1)}, f32[2048,1,128]{0,2,1:T(8,128)}, u32[]{:S(2)}) copy-start(f32[2048,1,128]{0,2,1:T(8,128)} %custom-call.1) | copy-start | bytes 3145732
  287.3 25.7 %all-to-all-start.8 = ((bf16[16,128,128]{2,1,0:T(8,128)(2,1)}), bf16[16,128,128]{2,1,0:T(8,128)(2,1)S(1)}, u32[]{:S(2)}, u32[]{:S(2)}) async-start(bf16[16,128,128]{2,1,0:T(8,128)(2,1)} %bitcast.37), calls=%async_computation.8 | async-start | bytes 1048576 | tf_op jit(solution)/shard_map/all_to_all | solution.py:207
  291.8 278.4 %all-gather.7.cloned.1.call-start = ((), (), s32[]{:S(2)}) async-start(), calls=%async_computation.17 | async-start | bytes 1114112 | tf_op jit(solution)/shard_map/all_gather | solution.py:222
  345.0 161.7 %all-to-all-start.7 = ((bf16[16,128,128]{2,1,0:T(8,128)(2,1)}), bf16[16,128,128]{2,1,0:T(8,128)(2,1)S(1)}, u32[]{:S(2)}, u32[]{:S(2)}) async-start(bf16[16,128,128]{2,1,0:T(8,128)(2,1)} %bitcast.34), calls=%async_computation.7 | async-start | bytes 1048576 | tf_op jit(solution)/shard_map/all_to_all | solution.py:206
  354.6 387.6 %all-reduce.3.cloned.1.call-start = ((), (), s32[]{:S(2)}) async-start(), calls=%async_computation.18 | async-start | bytes 917504 | tf_op jit(solution)/shard_map/psum | solution.py:223
  (18 other events, 58.5 us)
Sparse Core Ops, SparseCore 0:
  11.4 155.1 all-gather.4
  209.8 102.7 reduce-scatter.3
  315.3 97.4 reduce-scatter.7
  415.4 88.7 reduce-scatter.5
  507.1 63.0 all-gather.6
  572.9 169.1 all-reduce.2
